TPU v7x, 512 devices: a whole 4x8x8 slice. The times are simulated.
512 devices in a mesh: dp: 2 (over core), ctx: 64 (over z, y), head: 4 (over x).
Axes of the slice: x: 4, y: 8, z: 8, core: 2. Of those that a mesh axis runs over, the one named last changes fastest.
Arguments:
- queries: bfloat16 [2, 8192, 2560], P('dp', 'ctx', 'head'), may hold values from -25 to 25
- keys: bfloat16 [2, 8192, 2560], P('dp', 'ctx', 'head'), may hold values from -25 to 25
- values: bfloat16 [2, 8192, 2560], P('dp', 'ctx', 'head'), may hold values from -6 to 6
- grad_y: bfloat16 [2, 8192, 2560], P('dp', 'ctx', 'head'), may hold values from -6 to 6
- out_gain: float32 [2560], P('head'), may hold values from 0.1 to 1.9
- offsets: int32 [2, 20], P(None, 'head'), may hold values from 0 to 63, as said below
Outputs:
- attended: bfloat16 [2, 8192, 2560], P('dp', 'ctx', 'head')
- query_grad: bfloat16 [2, 8192, 2560], P('dp', 'ctx', 'head')
- key_grad: bfloat16 [2, 8192, 2560], P('dp', 'ctx', 'head')
- value_grad: bfloat16 [2, 8192, 2560], P('dp', 'ctx', 'head')
- gain_grad: float32 [2560], P('head')
Inputs may be any that keep to these rules, and one draw needn't show every extreme that they name: Row 0 holds offsets below 8, row 1 offsets below 64.
All inputs are finite; a program needn't handle non-finite values.
Results may differ from a plain program's by a relative error of at most 0.011.
Values may be sent and summed in bfloat16 or wider, within the bound.
A program may use at most 64 MiB of HBM per device.

v0:
```python
import math
import jax
import jax.numpy as jnp
from jax import lax
from jax.sharding import PartitionSpec as P

HEAD_DIM = 128
SPAN = 4
R1 = 8
EPS = 1e-06


def group_gather(block, axis, group):
    count = lax.axis_size(axis)
    pieces = [block]
    for shift in range(1, group):
        route = []
        for src in range(count):
            base = src - src % group
            route.append((src, base + (src % group + shift) % group))
        pieces.append(lax.ppermute(block, axis, route))
    return jnp.concatenate(pieces, 0)


def pick_rows(source_rows, dilation, shifts):
    row_count, head_count, head_width = source_rows.shape
    grouped = source_rows.reshape(row_count // dilation, dilation, head_count, head_width)
    hit_mask = jnp.arange(dilation, dtype=jnp.int32).reshape(1, dilation, 1, 1) == shifts.reshape(
        1, 1, head_count, 1
    )
    chosen = jnp.where(hit_mask, grouped, jnp.zeros((), source_rows.dtype))
    return jnp.sum(chosen, axis=1, dtype=source_rows.dtype)


def place_rows(row_values, dilation, shifts):
    row_count, head_count, head_width = row_values.shape
    hit_mask = jnp.arange(dilation, dtype=jnp.int32).reshape(1, dilation, 1, 1) == shifts.reshape(
        1, 1, head_count, 1
    )
    spread = jnp.where(hit_mask, row_values[:, None], jnp.zeros((), row_values.dtype))
    return spread.reshape(row_count * dilation, head_count, head_width)


def level_scores(q_rows, k_rows):
    score_scale = 1.0 / math.sqrt(q_rows.shape[-1])
    return (
        jnp.einsum("qhe,khe->hqk", q_rows, k_rows, preferred_element_type=jnp.float32) * score_scale
    )


def attend(q_rows, k_rows, v_rows):
    scores = level_scores(q_rows, k_rows)
    row_max = jnp.max(scores, axis=-1, keepdims=True)
    log_total = row_max[..., 0] + jnp.log(jnp.sum(jnp.exp(scores - row_max), axis=-1))
    soft_rows = jnp.exp(scores - log_total[..., None]).astype(jnp.bfloat16)
    level_out = jnp.einsum("hqk,khe->qhe", soft_rows, v_rows, preferred_element_type=jnp.float32)
    return (level_out, log_total.T)


def score_grads(q_rows, k_rows, v_rows, log_total, grad_low, row_shift):
    score_scale = 1.0 / math.sqrt(q_rows.shape[-1])
    scores = level_scores(q_rows, k_rows)
    exact_soft = jnp.exp(scores - log_total.T[..., None])
    prob_grad = jnp.einsum("qhe,khe->hqk", grad_low, v_rows, preferred_element_type=jnp.float32)
    score_grad = (exact_soft * (prob_grad + row_shift.T[..., None]) * score_scale).astype(
        jnp.bfloat16
    )
    return (score_grad, exact_soft.astype(jnp.bfloat16))


def key_parts(score_grad, soft_low, q_rows, grad_low):
    k_part = jnp.einsum("hqk,qhe->khe", score_grad, q_rows, preferred_element_type=jnp.float32)
    v_part = jnp.einsum("hqk,qhe->khe", soft_low, grad_low, preferred_element_type=jnp.float32)
    return (k_part, v_part)


def query_part(score_grad, k_rows):
    return jnp.einsum("hqk,khe->qhe", score_grad, k_rows, preferred_element_type=jnp.float32)


def split_qkv(packed, head_count):
    width = head_count * HEAD_DIM
    shape = (packed.shape[0], head_count, HEAD_DIM)
    return tuple((packed[:, i * width : (i + 1) * width].reshape(shape) for i in range(3)))


def pack_grads(grad_low, row_shift):
    rows = grad_low.shape[0]
    return jnp.concatenate(
        [grad_low.astype(jnp.float32).reshape(rows, -1), row_shift.astype(jnp.float32)], 1
    )


def unpack_grads(packed, head_count):
    width = head_count * HEAD_DIM
    grad_low = packed[:, :width].astype(jnp.bfloat16).reshape(-1, head_count, HEAD_DIM)
    return (grad_low, packed[:, width:])


def shards(queries, keys, values, grad_y, out_gain, offsets):
    tokens = queries.shape[1]
    flat_width = queries.shape[2]
    head_count = flat_width // HEAD_DIM
    row_shape = (tokens, head_count, HEAD_DIM)
    q_own = queries[0].reshape(row_shape)
    k_own = keys[0].reshape(row_shape)
    v_own = values[0].reshape(row_shape)
    ctx_size = lax.axis_size("ctx")
    my_place = lax.axis_index("ctx")
    mid_shift = offsets[0]
    top_shift = offsets[1]
    positions = jnp.arange(tokens, dtype=jnp.int32)
    mid_hit = (positions % R1)[:, None] == mid_shift[None, :]
    top_hit = (positions % ctx_size)[:, None] == top_shift[None, :]
    mid_pack = jnp.concatenate(
        [pick_rows(x, R1, mid_shift).reshape(-1, flat_width) for x in (q_own, k_own, v_own)], 1
    )
    top_pack = jnp.concatenate(
        [pick_rows(x, ctx_size, top_shift).reshape(-1, flat_width) for x in (q_own, k_own, v_own)],
        1,
    )
    mid_rows = mid_pack.shape[0]
    top_rows = top_pack.shape[0]
    mid_all = group_gather(mid_pack, "ctx", SPAN)
    top_all = lax.all_gather(top_pack, "ctx", axis=0, tiled=True)
    mid_q, mid_k, mid_v = split_qkv(mid_all, head_count)
    top_q, top_k, top_v = split_qkv(top_all, head_count)
    top_start = my_place * top_rows
    base_out, base_total = attend(q_own, k_own, v_own)
    mid_out_all, mid_total_all = attend(mid_q, mid_k, mid_v)
    top_out_all, top_total_all = attend(top_q, top_k, top_v)
    mid_out = mid_out_all[:mid_rows]
    mid_total = mid_total_all[:mid_rows]
    top_out = lax.dynamic_slice_in_dim(top_out_all, top_start, top_rows, 0)
    top_total = lax.dynamic_slice_in_dim(top_total_all, top_start, top_rows, 0)
    mid_full = place_rows(mid_total[..., None], R1, mid_shift)[..., 0]
    top_full = place_rows(top_total[..., None], ctx_size, top_shift)[..., 0]
    row_max = jnp.maximum(base_total, jnp.where(mid_hit, mid_full, base_total))
    row_max = jnp.maximum(row_max, jnp.where(top_hit, top_full, base_total))
    base_expo = jnp.exp(base_total - row_max)
    mid_expo = jnp.where(mid_hit, jnp.exp(mid_full - row_max), 0.0)
    top_expo = jnp.where(top_hit, jnp.exp(top_full - row_max), 0.0)
    denom = base_expo + mid_expo + top_expo
    base_share = base_expo / denom
    mid_share = mid_expo / denom
    top_share = top_expo / denom
    attn = (
        base_share[..., None] * base_out
        + mid_share[..., None] * place_rows(mid_out, R1, mid_shift)
        + top_share[..., None] * place_rows(top_out, ctx_size, top_shift)
    )
    inv_rms = lax.rsqrt(jnp.mean(attn * attn, axis=-1, keepdims=True) + EPS)
    normed = attn * inv_rms
    gain_rows = out_gain.reshape(head_count, HEAD_DIM)
    attended = (normed * gain_rows).astype(jnp.bfloat16).reshape(1, tokens, flat_width)
    grad_full = grad_y[0].reshape(row_shape).astype(jnp.float32)
    gain_part = jnp.sum(grad_full * normed, axis=0).reshape(flat_width)
    grad_norm = grad_full * gain_rows
    grad_attn = inv_rms * (
        grad_norm - normed * jnp.mean(grad_norm * normed, axis=-1, keepdims=True)
    )
    inner = jnp.sum(grad_attn * attn, axis=-1)
    base_low = (base_share[..., None] * grad_attn).astype(jnp.bfloat16)
    base_shift = -(base_share * inner)
    base_grad, base_soft = score_grads(q_own, k_own, v_own, base_total, base_low, base_shift)
    base_dq = query_part(base_grad, k_own)
    base_dk, base_dv = key_parts(base_grad, base_soft, q_own, base_low)
    mid_sel = pick_rows(mid_share[..., None], R1, mid_shift)[..., 0]
    mid_low = (mid_sel[..., None] * pick_rows(grad_attn, R1, mid_shift)).astype(jnp.bfloat16)
    mid_row_shift = -(mid_sel * pick_rows(inner[..., None], R1, mid_shift)[..., 0])
    top_sel = pick_rows(top_share[..., None], ctx_size, top_shift)[..., 0]
    top_low = (top_sel[..., None] * pick_rows(grad_attn, ctx_size, top_shift)).astype(jnp.bfloat16)
    top_row_shift = -(top_sel * pick_rows(inner[..., None], ctx_size, top_shift)[..., 0])
    mid_low_all, mid_shift_all = unpack_grads(
        group_gather(pack_grads(mid_low, mid_row_shift), "ctx", SPAN), head_count
    )
    top_grads = pack_grads(top_low, top_row_shift)
    gain_row = jnp.pad(gain_part, (0, top_grads.shape[1] - flat_width))[None]
    gathered = lax.all_gather(jnp.concatenate([top_grads, gain_row], 0), "ctx", axis=0)
    top_low_all, top_shift_all = unpack_grads(
        gathered[:, :top_rows].reshape(-1, top_grads.shape[1]), head_count
    )
    gain_grad = lax.psum(jnp.sum(gathered[:, top_rows, :flat_width], axis=0), "dp")
    mid_grad, mid_soft = score_grads(mid_q, mid_k, mid_v, mid_total_all, mid_low_all, mid_shift_all)
    mid_dq = query_part(mid_grad[:, :mid_rows], mid_k)
    mid_dk, mid_dv = key_parts(
        mid_grad[:, :, :mid_rows], mid_soft[:, :, :mid_rows], mid_q, mid_low_all
    )
    top_grad, top_soft = score_grads(top_q, top_k, top_v, top_total_all, top_low_all, top_shift_all)
    own_grad = lax.dynamic_slice_in_dim(top_grad, top_start, top_rows, 1)
    top_dq = query_part(own_grad, top_k)
    key_grad_cols = lax.dynamic_slice_in_dim(top_grad, top_start, top_rows, 2)
    key_soft_cols = lax.dynamic_slice_in_dim(top_soft, top_start, top_rows, 2)
    top_dk, top_dv = key_parts(key_grad_cols, key_soft_cols, top_q, top_low_all)
    query_grad = (
        base_dq + place_rows(mid_dq, R1, mid_shift) + place_rows(top_dq, ctx_size, top_shift)
    )
    key_grad = base_dk + place_rows(mid_dk, R1, mid_shift) + place_rows(top_dk, ctx_size, top_shift)
    value_grad = (
        base_dv + place_rows(mid_dv, R1, mid_shift) + place_rows(top_dv, ctx_size, top_shift)
    )
    out_shape = (1, tokens, flat_width)
    return (
        attended,
        query_grad.astype(jnp.bfloat16).reshape(out_shape),
        key_grad.astype(jnp.bfloat16).reshape(out_shape),
        value_grad.astype(jnp.bfloat16).reshape(out_shape),
        gain_grad,
    )


def solution(mesh):
    in_specs = (
        P("dp", "ctx", "head"),
        P("dp", "ctx", "head"),
        P("dp", "ctx", "head"),
        P("dp", "ctx", "head"),
        P("head"),
        P(None, "head"),
    )
    out_specs = (
        P("dp", "ctx", "head"),
        P("dp", "ctx", "head"),
        P("dp", "ctx", "head"),
        P("dp", "ctx", "head"),
        P("head"),
    )
    return jax.shard_map(shards, mesh=mesh, in_specs=in_specs, out_specs=out_specs, check_vma=False)
```

profile of v0, /device:TPU:1, one launch (start us, length us, event | category | flops | bytes accessed | tf_op | source)
XLA Modules:
  0.0 159.5 jit_solution(9887099655481750333)
XLA Ops:
  0.6 0.8 slice_bitcast_fusion.5
  1.5 1.5 fusion.24
  3.0 6.1 %collective-permute-start.2 = (bf16[16,1920]{1,0:T(8,128)(2,1)S(1)}, bf16[16,1920]{1,0:T(8,128)(2,1)S(1)}, u32[]{:S(2)}, u32[]{:S(2)}) collective-permute-start(bf16[16,1920]{1,0:T(8,128)(2,1)S(1)} %bitcast_dynamic-update-slice_fusion), channel_id=1, source_target_pairs={{0,12},{4,0},{8,4},{12,8},{16,28},{20,16},{24,20},{28,24},{32,44},... | collective-permute-start | bytes 184328 | tf_op jit(solution)/shard_map/ppermute | solution.py:21
  9.1 1.9 %collective-permute-start.1 = (bf16[16,1920]{1,0:T(8,128)(2,1)S(1)}, bf16[16,1920]{1,0:T(8,128)(2,1)S(1)}, u32[]{:S(2)}, u32[]{:S(2)}) collective-permute-start(bf16[16,1920]{1,0:T(8,128)(2,1)S(1)} %bitcast_dynamic-update-slice_fusion), channel_id=1, source_target_pairs={{0,8},{4,12},{8,0},{12,4},{16,24},{20,28},{24,16},{28,20},{32,40},... | collective-permute-start | bytes 184328 | tf_op jit(solution)/shard_map/ppermute | solution.py:21
  11.0 2.3 %collective-permute-start = (bf16[16,1920]{1,0:T(8,128)(2,1)S(1)}, bf16[16,1920]{1,0:T(8,128)(2,1)S(1)}, u32[]{:S(2)}, u32[]{:S(2)}) collective-permute-start(bf16[16,1920]{1,0:T(8,128)(2,1)S(1)} %bitcast_dynamic-update-slice_fusion), channel_id=1, source_target_pairs={{0,4},{4,8},{8,12},{12,0},{16,20},{20,24},{24,28},{28,16},{32,36},... | collective-permute-start | bytes 184328 | tf_op jit(solution)/shard_map/ppermute | solution.py:21
  13.6 0.7 copy-done.1
  14.5 0.7 copy-done.2
  16.4 0.3 copy-done.8
  17.4 44.2 %all-gather.1 = bf16[64,2,1920]{2,1,0:T(2,128)(2,1)S(1)} all-gather(bf16[1,2,1920]{2,1,0:T(2,128)(2,1)S(1)} %maximum_bitcast_fusion.2), channel_id=1, replica_groups=mesh['dp'=2,'ctx'=64,'head'=4] {'ctx'}, dimensions={0}, use_global_device_ids=true | all-gather | bytes 499200 | tf_op jit(solution)/shard_map/all_gather | solution.py:125
  65.3 0.5 multiply_reduce_fusion.3
  65.8 0.7 copy-done.9
  66.5 0.8 multiply_reduce_fusion.2
  68.2 0.6 pad_maximum_fusion.2
  68.9 3.9 %collective-permute-start.5 = (f32[16,645]{1,0:T(8,128)}, f32[16,645]{1,0:T(8,128)}, u32[]{:S(2)}, u32[]{:S(2)}) collective-permute-start(f32[16,645]{1,0:T(8,128)} %pad_maximum_fusion.2), channel_id=1, source_target_pairs={{0,12},{4,0},{8,4},{12,8},{16,28},{20,16},{24,20},{28,24},{32,44},... | collective-permute-start | bytes 123848 | tf_op jit(solution)/shard_map/ppermute | solution.py:21
  72.8 2.8 %collective-permute-start.4 = (f32[16,645]{1,0:T(8,128)}, f32[16,645]{1,0:T(8,128)}, u32[]{:S(2)}, u32[]{:S(2)}) collective-permute-start(f32[16,645]{1,0:T(8,128)} %pad_maximum_fusion.2), channel_id=1, source_target_pairs={{0,8},{4,12},{8,0},{12,4},{16,24},{20,28},{24,16},{28,20},{32,40},... | collective-permute-start | bytes 123848 | tf_op jit(solution)/shard_map/ppermute | solution.py:21
  75.6 1.9 %collective-permute-start.3 = (f32[16,645]{1,0:T(8,128)}, f32[16,645]{1,0:T(8,128)}, u32[]{:S(2)}, u32[]{:S(2)}) collective-permute-start(f32[16,645]{1,0:T(8,128)} %pad_maximum_fusion.2), channel_id=1, source_target_pairs={{0,4},{4,8},{8,12},{12,0},{16,20},{20,24},{24,28},{28,16},{32,36},... | collective-permute-start | bytes 123848 | tf_op jit(solution)/shard_map/ppermute | solution.py:21
  78.2 38.9 %all-gather.2 = f32[64,3,645]{2,1,0:T(4,128)S(1)} all-gather(f32[1,3,645]{2,1,0:T(4,128)S(1)} %maximum_bitcast_fusion.1), channel_id=2, replica_groups=mesh['dp'=2,'ctx'=64,'head'=4] {'ctx'}, dimensions={0}, use_global_device_ids=true | all-gather | bytes 503100 | tf_op jit(solution)/shard_map/all_gather | solution.py:179
  117.2 1.0 reshape.365
  118.2 0.8 slice_bitcast_fusion.3
  119.1 1.0 slice.110
  120.3 0.9 convolution_bitcast_fusion.9
  121.7 0.4 convolution_bitcast_fusion.8
  122.1 0.4 fusion.17
  122.7 0.7 copy-done.4
  123.5 0.8 copy.357
  124.5 28.0 %psum.7 = f32[640]{0:T(1024)} all-reduce(f32[640]{0:T(1024)S(1)} %slice_reduce_fusion), channel_id=1, replica_groups=mesh['dp'=2,'ctx'=64,'head'=4] {'dp'}, use_global_device_ids=true, to_apply=%region_23.24 | all-reduce | flops 640 | bytes 5120 | tf_op jit(solution)/shard_map/psum | solution.py:183
  152.5 0.9 pad_maximum_fusion.1
  153.4 0.9 convolution_bitcast_fusion.5
  154.2 0.8 maximum_bitcast_fusion
  156.1 0.8 copy.359
  157.4 0.8 copy.358
  158.7 0.8 copy.360
  (114 shorter events, 10.7 us)
Async XLA Ops:
  1.5 11.9 %copy-start = (bf16[1,128,640]{2,1,0:T(8,128)(2,1)S(1)}, bf16[1,128,640]{2,1,0:T(8,128)(2,1)}, u32[]{:S(2)}) copy-start(bf16[1,128,640]{2,1,0:T(8,128)(2,1)} %param.6) | copy-start | bytes 491524
  3.0 60.7 %collective-permute-start.2 = (bf16[16,1920]{1,0:T(8,128)(2,1)S(1)}, bf16[16,1920]{1,0:T(8,128)(2,1)S(1)}, u32[]{:S(2)}, u32[]{:S(2)}) collective-permute-start(bf16[16,1920]{1,0:T(8,128)(2,1)S(1)} %bitcast_dynamic-update-slice_fusion), channel_id=1, source_target_pairs={{0,12},{4,0},{8,4},{12,8},{16,28},{20,16},{24,20},{28,24},{32,44},... | collective-permute-start | bytes 184328 | tf_op jit(solution)/shard_map/ppermute | solution.py:21
  9.1 54.7 %collective-permute-start.1 = (bf16[16,1920]{1,0:T(8,128)(2,1)S(1)}, bf16[16,1920]{1,0:T(8,128)(2,1)S(1)}, u32[]{:S(2)}, u32[]{:S(2)}) collective-permute-start(bf16[16,1920]{1,0:T(8,128)(2,1)S(1)} %bitcast_dynamic-update-slice_fusion), channel_id=1, source_target_pairs={{0,8},{4,12},{8,0},{12,4},{16,24},{20,28},{24,16},{28,20},{32,40},... | collective-permute-start | bytes 184328 | tf_op jit(solution)/shard_map/ppermute | solution.py:21
  11.0 52.7 %collective-permute-start = (bf16[16,1920]{1,0:T(8,128)(2,1)S(1)}, bf16[16,1920]{1,0:T(8,128)(2,1)S(1)}, u32[]{:S(2)}, u32[]{:S(2)}) collective-permute-start(bf16[16,1920]{1,0:T(8,128)(2,1)S(1)} %bitcast_dynamic-update-slice_fusion), channel_id=1, source_target_pairs={{0,4},{4,8},{8,12},{12,0},{16,20},{20,24},{24,28},{28,16},{32,36},... | collective-permute-start | bytes 184328 | tf_op jit(solution)/shard_map/ppermute | solution.py:21
  13.4 0.9 copy-start.1
  14.3 0.9 copy-start.2
  15.8 0.9 copy-start.8
  62.7 0.7 copy-start.3
  63.8 0.6 copy-start.6
  64.1 0.6 copy-start.5
  65.8 0.7 copy-start.9
  68.9 83.7 %collective-permute-start.5 = (f32[16,645]{1,0:T(8,128)}, f32[16,645]{1,0:T(8,128)}, u32[]{:S(2)}, u32[]{:S(2)}) collective-permute-start(f32[16,645]{1,0:T(8,128)} %pad_maximum_fusion.2), channel_id=1, source_target_pairs={{0,12},{4,0},{8,4},{12,8},{16,28},{20,16},{24,20},{28,24},{32,44},... | collective-permute-start | bytes 123848 | tf_op jit(solution)/shard_map/ppermute | solution.py:21
  72.8 79.7 %collective-permute-start.4 = (f32[16,645]{1,0:T(8,128)}, f32[16,645]{1,0:T(8,128)}, u32[]{:S(2)}, u32[]{:S(2)}) collective-permute-start(f32[16,645]{1,0:T(8,128)} %pad_maximum_fusion.2), channel_id=1, source_target_pairs={{0,8},{4,12},{8,0},{12,4},{16,24},{20,28},{24,16},{28,20},{32,40},... | collective-permute-start | bytes 123848 | tf_op jit(solution)/shard_map/ppermute | solution.py:21
  75.6 76.9 %collective-permute-start.3 = (f32[16,645]{1,0:T(8,128)}, f32[16,645]{1,0:T(8,128)}, u32[]{:S(2)}, u32[]{:S(2)}) collective-permute-start(f32[16,645]{1,0:T(8,128)} %pad_maximum_fusion.2), channel_id=1, source_target_pairs={{0,4},{4,8},{8,12},{12,0},{16,20},{20,24},{24,28},{28,16},{32,36},... | collective-permute-start | bytes 123848 | tf_op jit(solution)/shard_map/ppermute | solution.py:21
  122.4 0.9 copy-start.4
  154.2 1.0 copy-start.7
where the time goes:
time: 160 us
  blocking collectives  111 us (69%)
  starting transfers between devices  19 us (12%)
  local copies, waits for them, and re-layouts  15.2 us (10%)
  other arithmetic  7.09 us (4%)
  matrix products  6.04 us (4%)
    all_gather x1, blocking collectives, shards(): top_all = lax.all_gather(top_pack, 'ctx', axis=0, tiled=True)  44.2 us
    all_gather x1, blocking collectives, shards(): lax.all_gather(jnp.concatenate([top_grads, gain_row], 0), 'ctx', axis=0)  38.9 us
    psum x1, blocking collectives, shards(): lax.psum(jnp.sum(gathered[:, top_rows, :flat_width], axis=0), 'dp')  28 us
    ppermute x6, starting transfers between devices, group_gather(): pieces.append(lax.ppermute(block, axis, route))  19 us
    unnamed x34, local copies, waits for them, and re-layouts  7.85 us
  transfers between devices with their start and end apart: 6, of which 0 were waited for; matrix products, arithmetic and copies ran while one was open for 7% of the time, Pallas kernels for 0%

commit v1 on v0

--- a/solution.py
+++ b/solution.py
@@ -122,7 +122,9 @@
     mid_rows = mid_pack.shape[0]
     top_rows = top_pack.shape[0]
     mid_all = group_gather(mid_pack, "ctx", SPAN)
-    top_all = lax.all_gather(top_pack, "ctx", axis=0, tiled=True)
+    top_all = jnp.concatenate(
+        lax.all_to_all(jnp.stack([top_pack] * lax.axis_size("ctx")), "ctx", 0, 0), axis=0
+    )
     mid_q, mid_k, mid_v = split_qkv(mid_all, head_count)
     top_q, top_k, top_v = split_qkv(top_all, head_count)
     top_start = my_place * top_rows

time: 160 us -> 135 us (0.84)
  blocking collectives: 111 us -> 55.8 us
  starting transfers between devices: 19 us -> 34.9 us
  waiting for transfers between devices: 0.02 us -> 11.6 us
  local copies, waits for them, and re-layouts: 15.2 us -> 17.4 us
    all_gather x1 -> x0, blocking collectives: 44.2 us -> none  [shards(): top_all = lax.all_gather(top_pack, 'ctx', axis=0, tiled=True)]
    all_to_all x0 -> x1, starting transfers between devices: none -> 14.6 us  [shards(): lax.all_to_all(jnp.stack([top_pack] * lax.axis_size('ctx')), 'ctx', 0, 0)]
    all_to_all x0 -> x1, waiting for transfers between devices: none -> 11.6 us  [shards(): lax.all_to_all(jnp.stack([top_pack] * lax.axis_size('ctx')), 'ctx', 0, 0)]
    psum x1, blocking collectives: 28 us -> 18.7 us  [shards(): lax.psum(jnp.sum(gathered[:, top_rows, :flat_width], axis=0), 'dp')]
    all_gather x1, blocking collectives: 38.9 us -> 37.1 us  [shards(): lax.all_gather(jnp.concatenate([top_grads, gain_row], 0), 'ctx', axis=0)]
    unnamed x34 -> x49, local copies, waits for them, and re-layouts: 7.85 us -> 8.77 us
  transfers between devices with their start and end apart: 6 -> 7, of which waited for: 0 -> 1; matrix products, arithmetic and copies ran while one was open for 7% -> 9% of each run, Pallas kernels for 0% -> 0%
where the time goes in v1:
time: 135 us
  blocking collectives  55.8 us (41%)
  starting transfers between devices  34.9 us (26%)
  local copies, waits for them, and re-layouts  17.4 us (13%)
  waiting for transfers between devices  11.6 us (9%)
  other arithmetic  7.6 us (6%)
  matrix products  6.05 us (4%)
    all_gather x1, blocking collectives, shards(): lax.all_gather(jnp.concatenate([top_grads, gain_row], 0), 'ctx', axis=0)  37.1 us
    ppermute x6, starting transfers between devices, group_gather(): pieces.append(lax.ppermute(block, axis, route))  20.3 us
    psum x1, blocking collectives, shards(): lax.psum(jnp.sum(gathered[:, top_rows, :flat_width], axis=0), 'dp')  18.7 us
    all_to_all x1, starting transfers between devices, shards(): lax.all_to_all(jnp.stack([top_pack] * lax.axis_size('ctx')), 'ctx', 0, 0)  14.6 us
    all_to_all x1, waiting for transfers between devices, shards(): lax.all_to_all(jnp.stack([top_pack] * lax.axis_size('ctx')), 'ctx', 0, 0)  11.6 us
    unnamed x49, local copies, waits for them, and re-layouts  8.77 us
  transfers between devices with their start and end apart: 7, of which 1 were waited for; matrix products, arithmetic and copies ran while one was open for 9% of the time, Pallas kernels for 0%

profile of v1, /device:TPU:1, one launch (start us, length us, event | category | flops | bytes accessed | tf_op | source)
XLA Modules:
  0.0 134.6 jit_solution(4235532540895969994)
XLA Ops:
  0.6 0.8 slice_bitcast_fusion.5
  1.4 0.5 copy-done.12
  2.0 1.5 %fusion.24 = (bf16[16,5,128]{2,0,1:T(8,128)(2,1)S(1)}, bf16[16,5,128]{2,0,1:T(8,128)(2,1)S(1)}, bf16[16,5,128]{2,0,1:T(8,128)(2,1)S(1)}) fusion(pred[8,5]{0,1:T(8,128)(4,1)S(1)} %iota_compare_fusion.1, bf16[1,128,640]{2,1,0:T(8,128)(2,1)} %param.6, bf16[1,128,640]{2,1,0:T(8,128)(2,1)} %param.7, bf16[1,128,640]{2,1,0:T(8,128)(2,1)} %param.8), kind=kLoop, calls=%fused_computation.70 | loop fusion | flops 460800 | bytes 553000 | tf_op jit(solution)/shard_map/reduce_sum | solution.py:32
  3.6 6.2 %collective-permute-start.2 = (bf16[16,1920]{1,0:T(8,128)(2,1)S(1)}, bf16[16,1920]{1,0:T(8,128)(2,1)S(1)}, u32[]{:S(2)}, u32[]{:S(2)}) collective-permute-start(bf16[16,1920]{1,0:T(8,128)(2,1)S(1)} %bitcast_dynamic-update-slice_fusion), channel_id=1, source_target_pairs={{0,12},{4,0},{8,4},{12,8},{16,28},{20,16},{24,20},{28,24},{32,44},... | collective-permute-start | bytes 184328 | tf_op jit(solution)/shard_map/ppermute | solution.py:21
  9.8 1.9 %collective-permute-start.1 = (bf16[16,1920]{1,0:T(8,128)(2,1)S(1)}, bf16[16,1920]{1,0:T(8,128)(2,1)S(1)}, u32[]{:S(2)}, u32[]{:S(2)}) collective-permute-start(bf16[16,1920]{1,0:T(8,128)(2,1)S(1)} %bitcast_dynamic-update-slice_fusion), channel_id=1, source_target_pairs={{0,8},{4,12},{8,0},{12,4},{16,24},{20,28},{24,16},{28,20},{32,40},... | collective-permute-start | bytes 184328 | tf_op jit(solution)/shard_map/ppermute | solution.py:21
  11.7 2.3 %collective-permute-start = (bf16[16,1920]{1,0:T(8,128)(2,1)S(1)}, bf16[16,1920]{1,0:T(8,128)(2,1)S(1)}, u32[]{:S(2)}, u32[]{:S(2)}) collective-permute-start(bf16[16,1920]{1,0:T(8,128)(2,1)S(1)} %bitcast_dynamic-update-slice_fusion), channel_id=1, source_target_pairs={{0,4},{4,8},{8,12},{12,0},{16,20},{20,24},{24,28},{28,16},{32,36},... | collective-permute-start | bytes 184328 | tf_op jit(solution)/shard_map/ppermute | solution.py:21
  14.5 0.7 copy-done.2
  15.9 1.0 stack.2
  17.0 14.6 %all-to-all-start = ((bf16[64,2,1920]{2,1,0:T(2,128)(2,1)}), bf16[64,2,1920]{2,1,0:T(2,128)(2,1)S(1)}, u32[]{:S(2)}, u32[]{:S(2)}) async-start(bf16[64,2,1920]{2,1,0:T(2,128)(2,1)} %stack.2), calls=%async_computation | async-start | bytes 983040 | tf_op jit(solution)/shard_map/all_to_all | solution.py:126
  32.3 0.5 copy-done.8
  33.5 0.5 and_select_fusion
  35.2 11.6 %all-to-all-done = bf16[64,2,1920]{2,1,0:T(2,128)(2,1)S(1)} async-done(((bf16[64,2,1920]{2,1,0:T(2,128)(2,1)}), bf16[64,2,1920]{2,1,0:T(2,128)(2,1)S(1)}, u32[]{:S(2)}, u32[]{:S(2)}) %all-to-all-start) | async-done | bytes 491552 | tf_op jit(solution)/shard_map/all_to_all | solution.py:126
  50.3 0.7 copy-done.9
  51.0 0.8 multiply_reduce_fusion.2
  52.7 0.6 pad_maximum_fusion.2
  53.3 5.3 %collective-permute-start.5 = (f32[16,645]{1,0:T(8,128)}, f32[16,645]{1,0:T(8,128)}, u32[]{:S(2)}, u32[]{:S(2)}) collective-permute-start(f32[16,645]{1,0:T(8,128)} %pad_maximum_fusion.2), channel_id=1, source_target_pairs={{0,12},{4,0},{8,4},{12,8},{16,28},{20,16},{24,20},{28,24},{32,44},... | collective-permute-start | bytes 123848 | tf_op jit(solution)/shard_map/ppermute | solution.py:21
  58.6 1.9 %collective-permute-start.4 = (f32[16,645]{1,0:T(8,128)}, f32[16,645]{1,0:T(8,128)}, u32[]{:S(2)}, u32[]{:S(2)}) collective-permute-start(f32[16,645]{1,0:T(8,128)} %pad_maximum_fusion.2), channel_id=1, source_target_pairs={{0,8},{4,12},{8,0},{12,4},{16,24},{20,28},{24,16},{28,20},{32,40},... | collective-permute-start | bytes 123848 | tf_op jit(solution)/shard_map/ppermute | solution.py:21
  60.5 2.6 %collective-permute-start.3 = (f32[16,645]{1,0:T(8,128)}, f32[16,645]{1,0:T(8,128)}, u32[]{:S(2)}, u32[]{:S(2)}) collective-permute-start(f32[16,645]{1,0:T(8,128)} %pad_maximum_fusion.2), channel_id=1, source_target_pairs={{0,4},{4,8},{8,12},{12,0},{16,20},{20,24},{24,28},{28,16},{32,36},... | collective-permute-start | bytes 123848 | tf_op jit(solution)/shard_map/ppermute | solution.py:21
  64.2 37.1 %all-gather.1 = f32[64,3,645]{2,1,0:T(4,128)S(1)} all-gather(f32[1,3,645]{2,1,0:T(4,128)S(1)} %maximum_bitcast_fusion.1), channel_id=2, replica_groups=mesh['dp'=2,'ctx'=64,'head'=4] {'ctx'}, dimensions={0}, use_global_device_ids=true | all-gather | bytes 503100 | tf_op jit(solution)/shard_map/all_gather | solution.py:181
  101.5 1.0 reshape.371
  102.5 0.8 slice_bitcast_fusion.3
  103.3 1.0 slice.110
  104.6 0.9 convolution_bitcast_fusion.9
  106.9 0.7 copy-done.4
  107.8 0.8 copy.289
  108.8 18.7 %psum.7 = f32[640]{0:T(1024)} all-reduce(f32[640]{0:T(1024)S(1)} %slice_reduce_fusion), channel_id=1, replica_groups=mesh['dp'=2,'ctx'=64,'head'=4] {'dp'}, use_global_device_ids=true, to_apply=%region_23.24 | all-reduce | flops 640 | bytes 5120 | tf_op jit(solution)/shard_map/psum | solution.py:185
  127.5 0.9 pad_maximum_fusion.1
  128.4 0.9 convolution_bitcast_fusion.5
  129.3 0.8 maximum_bitcast_fusion
  131.2 0.8 copy.291
  132.4 0.8 copy.290
  133.7 0.8 copy.292
  (132 shorter events, 13.1 us)
Async XLA Ops:
  1.4 0.5 copy-start.12
  1.4 14.0 %copy-start.14 = (s32[5]{0:T(128)}, s32[5]{0:T(128)S(1)}, u32[]{:S(2)}) copy-start(s32[5]{0:T(128)S(1)} %get-tuple-element.57) | copy-start | bytes 64
  2.0 12.1 %copy-start = (bf16[1,128,640]{2,1,0:T(8,128)(2,1)S(1)}, bf16[1,128,640]{2,1,0:T(8,128)(2,1)}, u32[]{:S(2)}) copy-start(bf16[1,128,640]{2,1,0:T(8,128)(2,1)} %param.6) | copy-start | bytes 491524
  3.6 10.7 %copy-start.1 = (bf16[1,128,640]{2,1,0:T(8,128)(2,1)S(1)}, bf16[1,128,640]{2,1,0:T(8,128)(2,1)}, u32[]{:S(2)}) copy-start(bf16[1,128,640]{2,1,0:T(8,128)(2,1)} %param.7) | copy-start | bytes 491524
  3.6 30.5 %collective-permute-start.2 = (bf16[16,1920]{1,0:T(8,128)(2,1)S(1)}, bf16[16,1920]{1,0:T(8,128)(2,1)S(1)}, u32[]{:S(2)}, u32[]{:S(2)}) collective-permute-start(bf16[16,1920]{1,0:T(8,128)(2,1)S(1)} %bitcast_dynamic-update-slice_fusion), channel_id=1, source_target_pairs={{0,12},{4,0},{8,4},{12,8},{16,28},{20,16},{24,20},{28,24},{32,44},... | collective-permute-start | bytes 184328 | tf_op jit(solution)/shard_map/ppermute | solution.py:21
  9.8 24.3 %collective-permute-start.1 = (bf16[16,1920]{1,0:T(8,128)(2,1)S(1)}, bf16[16,1920]{1,0:T(8,128)(2,1)S(1)}, u32[]{:S(2)}, u32[]{:S(2)}) collective-permute-start(bf16[16,1920]{1,0:T(8,128)(2,1)S(1)} %bitcast_dynamic-update-slice_fusion), channel_id=1, source_target_pairs={{0,8},{4,12},{8,0},{12,4},{16,24},{20,28},{24,16},{28,20},{32,40},... | collective-permute-start | bytes 184328 | tf_op jit(solution)/shard_map/ppermute | solution.py:21
  11.7 22.3 %collective-permute-start = (bf16[16,1920]{1,0:T(8,128)(2,1)S(1)}, bf16[16,1920]{1,0:T(8,128)(2,1)S(1)}, u32[]{:S(2)}, u32[]{:S(2)}) collective-permute-start(bf16[16,1920]{1,0:T(8,128)(2,1)S(1)} %bitcast_dynamic-update-slice_fusion), channel_id=1, source_target_pairs={{0,4},{4,8},{8,12},{12,0},{16,20},{20,24},{24,28},{28,16},{32,36},... | collective-permute-start | bytes 184328 | tf_op jit(solution)/shard_map/ppermute | solution.py:21
  14.3 0.9 copy-start.2
  15.5 16.6 %copy-start.10 = (pred[64,5]{0,1:T(8,128)(4,1)}, pred[64,5]{0,1:T(8,128)(4,1)S(1)}, u32[]{:S(2)}) copy-start(pred[64,5]{0,1:T(8,128)(4,1)S(1)} %iota_compare_fusion) | copy-start | bytes 964
  17.0 29.9 %all-to-all-start = ((bf16[64,2,1920]{2,1,0:T(2,128)(2,1)}), bf16[64,2,1920]{2,1,0:T(2,128)(2,1)S(1)}, u32[]{:S(2)}, u32[]{:S(2)}) async-start(bf16[64,2,1920]{2,1,0:T(2,128)(2,1)} %stack.2), calls=%async_computation | async-start | bytes 983040 | tf_op jit(solution)/shard_map/all_to_all | solution.py:126
  31.9 0.9 copy-start.8
  34.1 0.6 copy-start.6
  34.6 0.6 copy-start.5
  48.0 0.6 copy-start.17
  48.0 1.5 %copy-start.3 = (bf16[5,128,128]{1,2,0:T(8,128)(2,1)}, bf16[5,128,128]{1,2,0:T(8,128)(2,1)S(1)}, u32[]{:S(2)}) copy-start(bf16[5,128,128]{1,2,0:T(8,128)(2,1)S(1)} %fusion.23) | copy-start | bytes 491524
  48.3 0.6 copy-start.13
  48.3 0.7 copy-start.15
  48.3 0.7 copy-start.16
  50.3 0.7 copy-start.9
  53.3 74.2 %collective-permute-start.5 = (f32[16,645]{1,0:T(8,128)}, f32[16,645]{1,0:T(8,128)}, u32[]{:S(2)}, u32[]{:S(2)}) collective-permute-start(f32[16,645]{1,0:T(8,128)} %pad_maximum_fusion.2), channel_id=1, source_target_pairs={{0,12},{4,0},{8,4},{12,8},{16,28},{20,16},{24,20},{28,24},{32,44},... | collective-permute-start | bytes 123848 | tf_op jit(solution)/shard_map/ppermute | solution.py:21
  58.6 68.9 %collective-permute-start.4 = (f32[16,645]{1,0:T(8,128)}, f32[16,645]{1,0:T(8,128)}, u32[]{:S(2)}, u32[]{:S(2)}) collective-permute-start(f32[16,645]{1,0:T(8,128)} %pad_maximum_fusion.2), channel_id=1, source_target_pairs={{0,8},{4,12},{8,0},{12,4},{16,24},{20,28},{24,16},{28,20},{32,40},... | collective-permute-start | bytes 123848 | tf_op jit(solution)/shard_map/ppermute | solution.py:21
  60.5 67.0 %collective-permute-start.3 = (f32[16,645]{1,0:T(8,128)}, f32[16,645]{1,0:T(8,128)}, u32[]{:S(2)}, u32[]{:S(2)}) collective-permute-start(f32[16,645]{1,0:T(8,128)} %pad_maximum_fusion.2), channel_id=1, source_target_pairs={{0,4},{4,8},{8,12},{12,0},{16,20},{20,24},{24,28},{28,16},{32,36},... | collective-permute-start | bytes 123848 | tf_op jit(solution)/shard_map/ppermute | solution.py:21
  63.2 0.7 copy-start.11
  106.7 0.9 copy-start.4
  129.3 1.0 copy-start.7
